TPU v7x, 32 devices: a whole 2x2x4 slice. The times are simulated.
32 devices in a mesh: wheel: 16 (over z, x, core), slab: 2 (over y).
Axes of the slice: x: 2, y: 2, z: 4, core: 2. Of those that a mesh axis runs over, the one named last changes fastest.
Arguments:
- krylov_block: float32 [2, 32, 3, 16, 512], P(None, 'wheel', None, None, 'slab'), may hold values from -6 to 6
- blade_class: int32 [32], P('wheel'), may hold values from 0 to 3
- neighbors: int32 [8, 512], P(None, 'slab'), may hold values from 0 to 511
- iface_rows: int32 [2, 128], P(None, 'slab'), may hold values from 0 to 255
- face_rows: int32 [2, 128], P(None, 'slab'), may hold values from 0 to 255
- stiffness: float32 [3, 3, 8, 512], P(None, None, None, 'slab'), may hold values from -1.25 to 1.25
- lumped_mass: float32 [3, 512], P(None, 'slab'), may hold values from 0.5 to 2
- precond: bfloat16 [16, 16, 384, 384], P('wheel', 'slab'), may hold values from -0.3125 to 0.3125
Outputs:
- preconditioned: float32 [16, 16, 16, 384], P('wheel', 'slab')
Inputs may be any that keep to these rules, and one draw needn't show every extreme that they name: `neighbors`: extended numbering: own nodes first (256), then 64 from the lower slab, 64 from the upper slab, 64 from the previous sector, 64 from the next sector.
All inputs are finite; a program needn't handle non-finite values.
Results may differ from a plain program's by a relative error of at most 0.0039.
Values may be sent and summed in bfloat16 or wider, within the bound.
No kernel may reach another device: no remote copies, remote signals or barrier semaphores. Data moves between devices by JAX's collectives and lax.ppermute only.
A program may use at most 64 MiB of HBM per device.

v0:
```python
import math
import jax
import jax.numpy as jnp
from jax import lax
from jax.sharding import PartitionSpec as P

GROUP = 32
damping_ratio = 0.5
gyro_rate = 0.8
shift_value = 0.3
class_step = 0.125


def extended_2(block, sides, width, periodic):
    for axis, dim in sides:
        count = lax.axis_size(axis)
        forward = [(i, i + 1) for i in range(count - 1)]
        if periodic:
            forward.append((count - 1, 0))
        backward = [(target, source) for source, target in forward]
        low = lax.ppermute(
            lax.slice_in_dim(block, block.shape[dim] - width, None, axis=dim), axis, forward
        )
        high = lax.ppermute(lax.slice_in_dim(block, 0, width, axis=dim), axis, backward)
        block = jnp.concatenate([low, block, high], axis=dim)
    return block


def basis(row_ids, col_ids, sectors_all):
    pair_id = row_ids[:, None] // 2
    part_id = row_ids[:, None] % 2
    sector_id = col_ids[None, :]
    phases = pair_id * sector_id % sectors_all
    angles = 2.0 * math.pi / sectors_all * phases.astype(jnp.float32)
    parity = (1 - 2 * (sector_id % 2)).astype(jnp.float32)
    edge_rows = jnp.where(
        part_id == 0, jnp.ones_like(angles), parity * jnp.ones_like(angles)
    ) * math.sqrt(1.0 / sectors_all)
    inner_rows = jnp.where(part_id == 0, jnp.cos(angles), jnp.sin(angles)) * math.sqrt(
        2.0 / sectors_all
    )
    return jnp.where(pair_id == 0, edge_rows, inner_rows)


def arrange(harmonic):
    pair_rows, states, comps, vectors, nodes = harmonic.shape
    shaped = harmonic.reshape(pair_rows // 2, 2, states, comps, vectors, nodes // GROUP, GROUP)
    shaped = shaped.transpose(0, 5, 4, 1, 2, 3, 6)
    return shaped.reshape(pair_rows // 2, nodes // GROUP, vectors, 4 * comps * GROUP)


def on_device(
    krylov_block, blade_class, neighbors, iface_rows, face_rows, stiffness, lumped_mass, precond
):
    displacement = krylov_block[0]
    velocity = krylov_block[1]
    moved_field = displacement + damping_ratio * velocity
    rim_width = iface_rows.shape[1]
    face_width = face_rows.shape[1]
    rims = jnp.concatenate(
        (
            jnp.take(moved_field, iface_rows[0], axis=3),
            jnp.take(moved_field, iface_rows[1], axis=3),
        ),
        axis=3,
    )
    rimmed = extended_2(rims.astype(jnp.bfloat16), (("slab", 3),), rim_width, False).astype(
        rims.dtype
    )
    from_lower = rimmed[..., :rim_width]
    from_upper = rimmed[..., 3 * rim_width :]
    left_face = jnp.take(moved_field, face_rows[0], axis=3)
    right_face = jnp.take(moved_field, face_rows[1], axis=3)
    edges = jnp.concatenate((left_face[0], right_face[-1]), axis=2)
    faced = extended_2(edges, (("wheel", 2),), face_width, True)
    from_prev = jnp.concatenate((faced[None, :, :, :face_width], right_face[:-1]), axis=0)
    from_next = jnp.concatenate((left_face[1:], faced[None, :, :, 3 * face_width :]), axis=0)
    extended = jnp.concatenate((moved_field, from_lower, from_upper, from_prev, from_next), axis=3)
    picked = jnp.take(extended, neighbors, axis=3)
    restore = jnp.einsum("cdkn,sdvkn->scvn", stiffness, picked, precision=lax.Precision.HIGHEST)
    scale = (1.0 + class_step * blade_class.astype(jnp.float32))[:, None, None, None]
    gyro = gyro_rate * jnp.stack(
        (
            -lumped_mass[0] * velocity[:, 1],
            lumped_mass[1] * velocity[:, 0],
            jnp.zeros_like(velocity[:, 2]),
        ),
        axis=1,
    )
    res_disp = velocity - shift_value * displacement
    res_velo = -scale * restore - gyro - shift_value * lumped_mass[None, :, None, :] * velocity
    residual = jnp.stack((res_disp, res_velo), axis=0)
    local_sectors = residual.shape[1]
    sectors_all = lax.axis_size("wheel") * local_sectors
    spread = lax.all_to_all(residual, "wheel", split_axis=4, concat_axis=1, tiled=True)
    table = basis(
        jnp.arange(sectors_all, dtype=jnp.int32),
        jnp.arange(sectors_all, dtype=jnp.int32),
        sectors_all,
    )
    transformed = jnp.einsum(
        "bs,tscvn->btcvn", table, spread, precision=lax.Precision.HIGHEST
    ).astype(jnp.bfloat16)
    harmonic = lax.all_to_all(transformed, "wheel", split_axis=0, concat_axis=4, tiled=True)
    lhs = arrange(harmonic)
    return jnp.einsum("pgvj,pgij->pgvi", lhs, precond, preferred_element_type=jnp.float32)


def solution(mesh):
    return jax.shard_map(
        on_device,
        mesh=mesh,
        in_specs=(
            P(None, "wheel", None, None, "slab"),
            P("wheel"),
            P(None, "slab"),
            P(None, "slab"),
            P(None, "slab"),
            P(None, None, None, "slab"),
            P(None, "slab"),
            P("wheel", "slab", None, None),
        ),
        out_specs=P("wheel", "slab", None, None),
        check_vma=False,
    )
```

profile of v0, /device:TPU:0, one launch (start us, length us, event | category | flops | bytes accessed | tf_op | source)
XLA Modules:
  0.0 120.3 jit_solution(17209610336945923455)
XLA Ops:
  0.0 1.1 bitcast_add_fusion
  1.6 1.4 %compare_and_fusion.4 = (pred[64]{0:T(512)(128)(4,1)}, s32[64]{0:T(128)S(1)}, pred[64]{0:T(512)(128)(4,1)}, s32[64]{0:T(128)}) fusion(s32[2,64]{1,0:T(2,128)} %param.13), kind=kLoop, calls=%fused_computation.77 | loop fusion | flops 768 | bytes 1152 | tf_op jit(solution)/shard_map/jit(_take)/and | solution.py:63
  4.5 1.4 %bitcast_convert_fusion.1 = bf16[2,3,16,64]{3,2,1,0:T(8,128)(2,1)} fusion(bf16[64,2,3,16]{0,3,2,1:T(8,128)(2,1)} %copy.156, pred[64]{0:T(512)(128)(4,1)} %get-tuple-element.10), kind=kLoop, calls=%fused_computation.26 | loop fusion | flops 6144 | bytes 24640 | tf_op jit(solution)/shard_map/slice | solution.py:22
  5.9 5.5 %collective-permute-start = (bf16[2,3,16,64]{3,2,1,0:T(8,128)(2,1)}, bf16[2,3,16,64]{3,2,1,0:T(8,128)(2,1)}, u32[]{:S(2)}, u32[]{:S(2)}) collective-permute-start(bf16[2,3,16,64]{3,2,1,0:T(8,128)(2,1)} %bitcast_convert_fusion.1), channel_id=1, source_target_pairs={{0,1},{2,3},{4,5},{6,7},{8,9},{10,11},{12,13},{14,15},{16,17},{18,... | collective-permute-start | bytes 36872 | tf_op jit(solution)/shard_map/ppermute | solution.py:21
  13.6 1.3 %bitcast_convert_fusion = bf16[2,3,16,64]{3,2,1,0:T(8,128)(2,1)} fusion(bf16[64,2,3,16]{0,3,2,1:T(8,128)(2,1)} %copy.158, pred[64]{0:T(512)(128)(4,1)} %get-tuple-element.28), kind=kLoop, calls=%fused_computation.25 | loop fusion | flops 6144 | bytes 24640 | tf_op jit(solution)/shard_map/slice | solution.py:24
  14.9 1.3 %collective-permute-start.1 = (bf16[2,3,16,64]{3,2,1,0:T(8,128)(2,1)}, bf16[2,3,16,64]{3,2,1,0:T(8,128)(2,1)}, u32[]{:S(2)}, u32[]{:S(2)}) collective-permute-start(bf16[2,3,16,64]{3,2,1,0:T(8,128)(2,1)} %bitcast_convert_fusion), channel_id=1, source_target_pairs={{1,0},{3,2},{5,4},{7,6},{9,8},{11,10},{13,12},{15,14},{17,16},{19,... | collective-permute-start | bytes 36872 | tf_op jit(solution)/shard_map/ppermute | solution.py:24
  17.0 1.5 %gather_fusion.3 = f32[64,2,3,16]{3,1,2,0:T(2,128)} fusion(f32[2,3,16,256]{2,0,3,1:T(2,128)S(1)} %copy.155, s32[1024]{0:T(1024)S(1)} %pad_clamp_fusion.1), kind=kCustom, calls=%fused_computation.2.clone | custom fusion | bytes 49408 | tf_op jit(solution)/shard_map/jit(_take)/gather | solution.py:73
  18.5 1.0 copy.160
  19.5 1.5 %gather_fusion.4 = f32[64,2,3,16]{3,1,2,0:T(2,128)} fusion(f32[2,3,16,256]{2,0,3,1:T(2,128)S(1)} %copy.155, s32[1024]{0:T(1024)S(1)} %pad_clamp_fusion), kind=kCustom, calls=%fused_computation.3.clone | custom fusion | bytes 49408 | tf_op jit(solution)/shard_map/jit(_take)/gather | solution.py:72
  21.0 1.0 copy.162
  22.0 3.7 %collective-permute-start.3 = (f32[3,16,64]{2,1,0:T(8,128)S(1)}, f32[3,16,64]{2,1,0:T(8,128)S(1)}, u32[]{:S(2)}, u32[]{:S(2)}) collective-permute-start(f32[3,16,64]{2,1,0:T(8,128)S(1)} %get-tuple-element.21), channel_id=1, source_target_pairs={{2,0},{4,2},{6,4},{8,6},{10,8},{12,10},{14,12},{16,14},{18,16},{20... | collective-permute-start | bytes 36872 | tf_op jit(solution)/shard_map/ppermute | solution.py:24
  27.8 2.2 %copy.173 = f32[3,3,8,256,1]{2,0,1,4,3:T(4,128)} copy(f32[3,3,8,256,1]{3,2,1,0,4:T(8,128)} %bitcast.88) | data formatting | bytes 147456 | tf_op args[5]
  30.3 0.9 maximum_convert_fusion
  31.9 2.1 %copy.163 = f32[2,3,16,512]{2,0,3,1:T(2,128)} copy(f32[2,3,16,512]{3,2,1,0:T(8,128)S(1)} %concatenate.18) | data formatting | bytes 393216 | tf_op jit(solution)/shard_map/concatenate | solution.py:78
  33.9 23.2 %gather_fusion = f32[2048,2,3,16]{3,1,2,0:T(2,128)} fusion(f32[2,3,16,512]{2,0,3,1:T(2,128)} %copy.163, s32[2048]{0:T(1024)S(1)} %broadcast_clamp_fusion), kind=kCustom, calls=%fused_computation.4 | custom fusion | bytes 1581056 | tf_op jit(solution)/shard_map/jit(_take)/gather | solution.py:79
  57.1 10.7 %fusion.6 = f32[256,2,16,3]{2,3,1,0:T(4,128)S(1)} fusion(f32[3,3,8,256,1]{2,0,1,4,3:T(4,128)} %copy.173, f32[8,256,2,3,16]{4,2,3,1,0:T(2,128)} %bitcast.80, pred[8,256]{0,1:T(8,128)(4,1)S(1)} %copy.154), kind=kOutput, calls=%fused_computation.12 | convolution fusion | flops 7274496 | bytes 960512 | tf_op jit(solution)/shard_map/cdkn,sdvkn->scvn/dot_general | solution.py:80
  68.3 1.0 fusion.14
  69.3 0.9 pad_maximum_fusion
  70.2 2.2 %copy.167 = f32[2,2,3,16,256]{3,1,2,0,4:T(2,128)} copy(f32[2,2,3,16,256]{4,3,2,1,0:T(8,128)S(1)} %pad_maximum_fusion) | data formatting | bytes 393216 | tf_op jit(solution)/shard_map/stack | solution.py:92
  72.3 4.2 %reshape.174 = f32[16,1,3072]{2,1,0:T(1,128)} reshape(f32[256,2,3,2,16]{4,3,2,1,0:T(2,128)} %bitcast.81) | data formatting | bytes 393216
  76.6 5.4 %all-to-all-start = ((f32[16,1,3072]{2,1,0:T(1,128)}), f32[16,1,3072]{2,1,0:T(1,128)S(1)}, u32[]{:S(2)}, u32[]{:S(2)}) async-start(f32[16,1,3072]{2,1,0:T(1,128)} %reshape.174), calls=%async_computation | async-start | bytes 393216 | tf_op jit(solution)/shard_map/all_to_all | solution.py:95
  82.0 8.9 %all-to-all-done = f32[16,1,3072]{2,1,0:T(1,128)S(1)} async-done(((f32[16,1,3072]{2,1,0:T(1,128)}), f32[16,1,3072]{2,1,0:T(1,128)S(1)}, u32[]{:S(2)}, u32[]{:S(2)}) %all-to-all-start) | async-done | bytes 196640 | tf_op jit(solution)/shard_map/all_to_all | solution.py:95
  91.4 1.1 reduce
  92.5 3.3 %reshape.175 = f32[256,2,3,2,16]{4,3,2,1,0:T(2,128)} reshape(f32[16,3072]{1,0:T(8,128)S(1)} %reduce) | data formatting | bytes 393216
  95.8 3.7 %copy.168 = f32[2,2,3,16,16,16]{5,3,2,1,4,0:T(8,128)} copy(f32[2,2,3,16,16,16]{3,1,2,0,5,4:T(2,128)} %bitcast.82) | data formatting | bytes 393216 | tf_op jit(solution)/shard_map/all_to_all | solution.py:95
  99.5 2.0 %copy.169 = f32[2,32,3,16,16]{1,4,3,2,0:T(8,128)S(1)} copy(f32[2,32,3,16,16]{4,3,2,1,0:T(8,128)} %bitcast.83) | data formatting | bytes 393216 | tf_op jit(solution)/shard_map/all_to_all | solution.py:95
  101.4 0.9 fusion.18
  102.4 1.3 %copy.170 = bf16[32,2,3,16,16]{4,3,2,1,0:T(8,128)(2,1)S(1)} copy(bf16[32,2,3,16,16]{0,4,3,2,1:T(8,128)(2,1)S(1)} %convert_element_type.25) | data formatting | bytes 196608 | tf_op jit(solution)/shard_map/convert_element_type | solution.py:103
  104.5 10.0 %all_to_all.33 = bf16[16,2,1536]{2,1,0:T(2,128)(2,1)S(1)} all-to-all(bf16[16,2,1536]{2,1,0:T(2,128)(2,1)S(1)} %reshape.176), channel_id=1, replica_groups=mesh['wheel'=16,'slab'=2] {'wheel'}, dimensions={0} | all-to-all | bytes 196608 | tf_op jit(solution)/shard_map/all_to_all | solution.py:104
  115.0 1.4 %copy.171 = bf16[2,2,3,16,16,16]{5,4,3,2,1,0:T(8,128)(2,1)} copy(bf16[2,2,3,16,16,16]{5,3,2,1,0,4:T(8,128)(2,1)S(1)} %bitcast.85) | data formatting | bytes 196608 | tf_op jit(solution)/shard_map/all_to_all | solution.py:104
  116.4 1.7 %reshape.112 = bf16[1,2,2,3,16,8,32]{6,5,4,3,2,1,0:T(8,128)(2,1)S(1)} reshape(bf16[2,2,3,16,16,16]{5,4,3,2,1,0:T(8,128)(2,1)} %copy.171) | data formatting | bytes 196608 | tf_op jit(solution)/shard_map/reshape | solution.py:47
  118.8 1.5 %fusion.9 = f32[1,8,16,384]{3,2,1,0:T(8,128)} fusion(bf16[8,16,384]{2,1,0:T(8,128)(2,1)S(1)} %reshape.113, bf16[1,8,384,384]{3,2,1,0:T(8,128)(2,1)S(1)} %copy-done), kind=kOutput, calls=%fused_computation.13 | convolution fusion | flops 37748736 | bytes 2654208 | tf_op jit(solution)/shard_map/pgvj,pgij->pgvi/dot_general | solution.py:106
  (50 shorter events, 10.9 us)
Async XLA Ops:
  0.0 118.8 %copy-start = (bf16[1,8,384,384]{3,2,1,0:T(8,128)(2,1)S(1)}, bf16[1,8,384,384]{3,2,1,0:T(8,128)(2,1)}, u32[]{:S(2)}) copy-start(bf16[1,8,384,384]{3,2,1,0:T(8,128)(2,1)} %param.17) | copy-start | bytes 7077892
  0.0 25.8 %copy-start.1 = (f32[2,2,3,16,256]{4,3,2,1,0:T(8,128)S(1)}, f32[2,2,3,16,256]{4,3,2,1,0:T(8,128)}, u32[]{:S(2)}) copy-start(f32[2,2,3,16,256]{4,3,2,1,0:T(8,128)} %param.10) | copy-start | bytes 589828
  0.0 25.8 %copy-start.2 = (s32[8,256]{1,0:T(8,128)S(1)}, s32[8,256]{1,0:T(8,128)}, u32[]{:S(2)}) copy-start(s32[8,256]{1,0:T(8,128)} %param.12) | copy-start | bytes 24580
  0.0 26.5 %copy-start.3 = (f32[3,256]{1,0:T(4,128)S(1)}, f32[3,256]{1,0:T(4,128)}, u32[]{:S(2)}) copy-start(f32[3,256]{1,0:T(4,128)} %param.16) | copy-start | bytes 9220
  5.9 24.4 %collective-permute-start = (bf16[2,3,16,64]{3,2,1,0:T(8,128)(2,1)}, bf16[2,3,16,64]{3,2,1,0:T(8,128)(2,1)}, u32[]{:S(2)}, u32[]{:S(2)}) collective-permute-start(bf16[2,3,16,64]{3,2,1,0:T(8,128)(2,1)} %bitcast_convert_fusion.1), channel_id=1, source_target_pairs={{0,1},{2,3},{4,5},{6,7},{8,9},{10,11},{12,13},{14,15},{16,17},{18,... | collective-permute-start | bytes 36872 | tf_op jit(solution)/shard_map/ppermute | solution.py:21
  14.9 15.4 %collective-permute-start.1 = (bf16[2,3,16,64]{3,2,1,0:T(8,128)(2,1)}, bf16[2,3,16,64]{3,2,1,0:T(8,128)(2,1)}, u32[]{:S(2)}, u32[]{:S(2)}) collective-permute-start(bf16[2,3,16,64]{3,2,1,0:T(8,128)(2,1)} %bitcast_convert_fusion), channel_id=1, source_target_pairs={{1,0},{3,2},{5,4},{7,6},{9,8},{11,10},{13,12},{15,14},{17,16},{19,... | collective-permute-start | bytes 36872 | tf_op jit(solution)/shard_map/ppermute | solution.py:24
  22.0 9.2 %collective-permute-start.3 = (f32[3,16,64]{2,1,0:T(8,128)S(1)}, f32[3,16,64]{2,1,0:T(8,128)S(1)}, u32[]{:S(2)}, u32[]{:S(2)}) collective-permute-start(f32[3,16,64]{2,1,0:T(8,128)S(1)} %get-tuple-element.21), channel_id=1, source_target_pairs={{2,0},{4,2},{6,4},{8,6},{10,8},{12,10},{14,12},{16,14},{18,16},{20... | collective-permute-start | bytes 36872 | tf_op jit(solution)/shard_map/ppermute | solution.py:24
  25.8 5.9 %collective-permute-start.2 = (f32[3,16,64]{2,1,0:T(8,128)S(1)}, f32[3,16,64]{2,1,0:T(8,128)S(1)}, u32[]{:S(2)}, u32[]{:S(2)}) collective-permute-start(f32[3,16,64]{2,1,0:T(8,128)S(1)} %get-tuple-element.22), channel_id=1, source_target_pairs={{0,2},{2,4},{4,6},{6,8},{8,10},{10,12},{12,14},{14,16},{16,18},{18... | collective-permute-start | bytes 36872 | tf_op jit(solution)/shard_map/ppermute | solution.py:21
  76.6 14.3 %all-to-all-start = ((f32[16,1,3072]{2,1,0:T(1,128)}), f32[16,1,3072]{2,1,0:T(1,128)S(1)}, u32[]{:S(2)}, u32[]{:S(2)}) async-start(f32[16,1,3072]{2,1,0:T(1,128)} %reshape.174), calls=%async_computation | async-start | bytes 393216 | tf_op jit(solution)/shard_map/all_to_all | solution.py:95
where the time goes:
time: 121 us; the launch traced here: 120 us
  local copies, waits for them, and re-layouts  59 us (49%)
  starting transfers between devices  15.9 us (13%)
  matrix products  13.1 us (11%)
  other arithmetic  12.6 us (10%)
  blocking collectives  9.96 us (8%)
  waiting for transfers between devices  9.41 us (8%)
    gather x1, local copies, waits for them, and re-layouts, on_device(): picked = jnp.take(extended, neighbors, axis=3)  23.2 us
    unnamed x14, local copies, waits for them, and re-layouts  11.1 us
    dot_general x1, matrix products, on_device(): jnp.einsum('cdkn,sdvkn->scvn', stiffness, picked, precision=lax.Precision...  10.7 us
    all_to_all x1, blocking collectives, on_device(): lax.all_to_all(transformed, 'wheel', split_axis=0, concat_axis=4, tiled=T...  9.96 us
    all_to_all x1, waiting for transfers between devices, on_device(): lax.all_to_all(residual, 'wheel', split_axis=4, concat_axis=1, tiled=True)  8.93 us
    all_to_all x3, local copies, waits for them, and re-layouts, on_device(): lax.all_to_all(residual, 'wheel', split_axis=4, concat_axis=1, tiled=True)  6.2 us
    ppermute x2, starting transfers between devices, extended_2(): lax.ppermute(lax.slice_in_dim(block, block.shape[dim] - width, None, axis...  5.49 us
    all_to_all x1, starting transfers between devices, on_device(): lax.all_to_all(residual, 'wheel', split_axis=4, concat_axis=1, tiled=True)  5.36 us
  transfers between devices with their start and end apart: 5, of which 2 were waited for; matrix products, arithmetic and copies ran while one was open for 12% of the time, Pallas kernels for 0%

commit v1 on v0

--- a/solution.py
+++ b/solution.py
@@ -101,7 +101,12 @@
     transformed = jnp.einsum(
         "bs,tscvn->btcvn", table, spread, precision=lax.Precision.HIGHEST
     ).astype(jnp.bfloat16)
-    harmonic = lax.all_to_all(transformed, "wheel", split_axis=0, concat_axis=4, tiled=True)
+    harmonic = jnp.concatenate(
+        lax.all_to_all(
+            jnp.stack(jnp.split(transformed, lax.axis_size("wheel"), axis=0)), "wheel", 0, 0
+        ),
+        axis=4,
+    )
     lhs = arrange(harmonic)
     return jnp.einsum("pgvj,pgij->pgvi", lhs, precond, preferred_element_type=jnp.float32)
 

time: 121 us -> 180 us (1.49); the launches traced: 120 us -> 177 us
  local copies, waits for them, and re-layouts: 59 us -> 117 us
    another operation x1 -> x20, local copies, waits for them, and re-layouts: 0.32 us -> 39.1 us  [the longest x18 37.1 us: on_device(): jnp.stack(jnp.split(transformed, lax.axis_size('wheel'), axis=0))]
    unnamed x14 -> x29, local copies, waits for them, and re-layouts: 11.1 us -> 32.7 us
  transfers between devices with their start and end apart: 5 -> 5, of which waited for: 2 -> 1; matrix products, arithmetic and copies ran while one was open for 12% -> 9% of each run, Pallas kernels for 0% -> 0%
where the time goes in v1:
time: 180 us; the launch traced here: 177 us
  local copies, waits for them, and re-layouts  117 us (65%)
  starting transfers between devices  15 us (8%)
  other arithmetic  13.3 us (7%)
  matrix products  13.1 us (7%)
  blocking collectives  9.96 us (6%)
  waiting for transfers between devices  8.73 us (5%)
    another operation x18, local copies, waits for them, and re-layouts, on_device(): jnp.stack(jnp.split(transformed, lax.axis_size('wheel'), axis=0))  37.1 us
    unnamed x29, local copies, waits for them, and re-layouts  32.7 us
    gather x1, local copies, waits for them, and re-layouts, on_device(): picked = jnp.take(extended, neighbors, axis=3)  23.1 us
    dot_general x1, matrix products, on_device(): jnp.einsum('cdkn,sdvkn->scvn', stiffness, picked, precision=lax.Precision...  10.7 us
    all_to_all x1, blocking collectives, on_device(): lax.all_to_all(jnp.stack(jnp.split(transformed, lax.axis_size('wheel'), a...  9.96 us
    all_to_all x1, waiting for transfers between devices, on_device(): lax.all_to_all(residual, 'wheel', split_axis=4, concat_axis=1, tiled=True)  8.72 us
    all_to_all x3, local copies, waits for them, and re-layouts, on_device(): lax.all_to_all(residual, 'wheel', split_axis=4, concat_axis=1, tiled=True)  6.21 us
    ppermute x2, starting transfers between devices, extended_2(): lax.ppermute(lax.slice_in_dim(block, 0, width, axis=dim), axis, backward)  5.77 us
  transfers between devices with their start and end apart: 5, of which 1 were waited for; matrix products, arithmetic and copies ran while one was open for 9% of the time, Pallas kernels for 0%

profile of v1, /device:TPU:0, one launch (start us, length us, event | category | flops | bytes accessed | tf_op | source)
XLA Modules:
  0.0 177.3 jit_solution(11596601320732432692)
XLA Ops:
  5.8 5.5 %collective-permute-start = (bf16[2,3,16,64]{3,2,1,0:T(8,128)(2,1)}, bf16[2,3,16,64]{3,2,1,0:T(8,128)(2,1)}, u32[]{:S(2)}, u32[]{:S(2)}) collective-permute-start(bf16[2,3,16,64]{3,2,1,0:T(8,128)(2,1)} %bitcast_convert_fusion.1), channel_id=1, source_target_pairs={{0,1},{2,3},{4,5},{6,7},{8,9},{10,11},{12,13},{14,15},{16,17},{18,... | collective-permute-start | bytes 36872 | tf_op jit(solution)/shard_map/ppermute | solution.py:21
  16.9 1.5 gather_fusion.3
  20.0 1.5 gather_fusion.4
  22.6 4.5 %collective-permute-start.3 = (f32[3,16,64]{2,1,0:T(8,128)S(1)}, f32[3,16,64]{2,1,0:T(8,128)S(1)}, u32[]{:S(2)}, u32[]{:S(2)}) collective-permute-start(f32[3,16,64]{2,1,0:T(8,128)S(1)} %get-tuple-element.37), channel_id=1, source_target_pairs={{2,0},{4,2},{6,4},{8,6},{10,8},{12,10},{14,12},{16,14},{18,16},{20... | collective-permute-start | bytes 36872 | tf_op jit(solution)/shard_map/ppermute | solution.py:24
  29.1 2.2 %copy.262 = f32[3,3,8,256,1]{2,0,1,4,3:T(4,128)} copy(f32[3,3,8,256,1]{3,2,1,0,4:T(8,128)} %bitcast.118) | data formatting | bytes 147456 | tf_op args[5]
  33.4 2.1 %copy.237 = f32[2,3,16,512]{2,0,3,1:T(2,128)} copy(f32[2,3,16,512]{3,2,1,0:T(8,128)S(1)} %concatenate.18) | data formatting | bytes 393216 | tf_op jit(solution)/shard_map/concatenate | solution.py:78
  35.5 23.1 %gather_fusion = f32[2048,2,3,16]{3,1,2,0:T(2,128)} fusion(f32[2,3,16,512]{2,0,3,1:T(2,128)} %copy.237, s32[2048]{0:T(1024)S(1)} %broadcast_clamp_fusion), kind=kCustom, calls=%fused_computation.4 | custom fusion | bytes 1581056 | tf_op jit(solution)/shard_map/jit(_take)/gather | solution.py:79
  58.6 10.7 %fusion.6 = f32[256,2,16,3]{2,3,1,0:T(4,128)S(1)} fusion(f32[3,3,8,256,1]{2,0,1,4,3:T(4,128)} %copy.262, f32[8,256,2,3,16]{4,2,3,1,0:T(2,128)} %bitcast.110, pred[8,256]{0,1:T(8,128)(4,1)S(1)} %copy.228), kind=kOutput, calls=%fused_computation.12 | convolution fusion | flops 7274496 | bytes 960512 | tf_op jit(solution)/shard_map/cdkn,sdvkn->scvn/dot_general | solution.py:80
  71.7 2.1 %copy.241 = f32[2,2,3,16,256]{3,1,2,0,4:T(2,128)} copy(f32[2,2,3,16,256]{4,3,2,1,0:T(8,128)S(1)} %pad_maximum_fusion) | data formatting | bytes 393216 | tf_op jit(solution)/shard_map/stack | solution.py:92
  73.8 4.2 %reshape.173 = f32[16,1,3072]{2,1,0:T(1,128)} reshape(f32[256,2,3,2,16]{4,3,2,1,0:T(2,128)} %bitcast.111) | data formatting | bytes 393216
  78.0 3.7 %all-to-all-start = ((f32[16,1,3072]{2,1,0:T(1,128)}), f32[16,1,3072]{2,1,0:T(1,128)S(1)}, u32[]{:S(2)}, u32[]{:S(2)}) async-start(f32[16,1,3072]{2,1,0:T(1,128)} %reshape.173), calls=%async_computation | async-start | bytes 393216 | tf_op jit(solution)/shard_map/all_to_all | solution.py:95
  81.8 8.7 %all-to-all-done = f32[16,1,3072]{2,1,0:T(1,128)S(1)} async-done(((f32[16,1,3072]{2,1,0:T(1,128)}), f32[16,1,3072]{2,1,0:T(1,128)S(1)}, u32[]{:S(2)}, u32[]{:S(2)}) %all-to-all-start) | async-done | bytes 196640 | tf_op jit(solution)/shard_map/all_to_all | solution.py:95
  92.1 3.3 %reshape.174 = f32[256,2,3,2,16]{4,3,2,1,0:T(2,128)} reshape(f32[16,3072]{1,0:T(8,128)S(1)} %reduce) | data formatting | bytes 393216
  95.4 3.7 %copy.242 = f32[2,2,3,16,16,16]{5,3,2,1,4,0:T(8,128)} copy(f32[2,2,3,16,16,16]{3,1,2,0,5,4:T(2,128)} %bitcast.112) | data formatting | bytes 393216 | tf_op jit(solution)/shard_map/all_to_all | solution.py:95
  99.1 2.0 %copy.243 = f32[2,32,3,16,16]{1,4,3,2,0:T(8,128)S(1)} copy(f32[2,32,3,16,16]{4,3,2,1,0:T(8,128)} %bitcast.113) | data formatting | bytes 393216 | tf_op jit(solution)/shard_map/all_to_all | solution.py:95
  102.0 3.9 %slice_bitcast_fusion = (bf16[1,2,2,3,16,16]{1,5,4,3,2,0:T(8,128)(2,1)S(1)}, bf16[1,2,2,3,16,16]{1,5,4,3,2,0:T(8,128)(2,1)S(1)}, bf16[1,2,2,3,16,16]{1,5,4,3,2,0...) fusion(bf16[32,2,3,16,16]{0,4,3,2,1:T(8,128)(2,1)S(1)} %convert, ...), kind=kLoop, calls=%fused_computation.14 | loop fusion | bytes 196608 | tf_op jit(solution)/shard_map/stack | solution.py:106
  105.9 2.3 %copy.244 = bf16[1,2,2,3,16,16]{5,4,3,2,1,0:T(8,128)(2,1)} copy(bf16[1,2,2,3,16,16]{1,5,4,3,2,0:T(8,128)(2,1)} %get-tuple-element.29) | data formatting | bytes 12288 | tf_op jit(solution)/shard_map/stack | solution.py:106
  109.7 2.3 %copy.245 = bf16[1,2,2,3,16,16]{5,4,3,2,1,0:T(8,128)(2,1)} copy(bf16[1,2,2,3,16,16]{1,5,4,3,2,0:T(8,128)(2,1)} %get-tuple-element.28) | data formatting | bytes 12288 | tf_op jit(solution)/shard_map/stack | solution.py:106
  112.0 2.3 %copy.246 = bf16[1,2,2,3,16,16]{5,4,3,2,1,0:T(8,128)(2,1)} copy(bf16[1,2,2,3,16,16]{1,5,4,3,2,0:T(8,128)(2,1)} %get-tuple-element.27) | data formatting | bytes 12288 | tf_op jit(solution)/shard_map/stack | solution.py:106
  114.2 2.3 %copy.247 = bf16[1,2,2,3,16,16]{5,4,3,2,1,0:T(8,128)(2,1)} copy(bf16[1,2,2,3,16,16]{1,5,4,3,2,0:T(8,128)(2,1)} %get-tuple-element.26) | data formatting | bytes 12288 | tf_op jit(solution)/shard_map/stack | solution.py:106
  116.5 2.3 %copy.248 = bf16[1,2,2,3,16,16]{5,4,3,2,1,0:T(8,128)(2,1)} copy(bf16[1,2,2,3,16,16]{1,5,4,3,2,0:T(8,128)(2,1)} %get-tuple-element.25) | data formatting | bytes 12288 | tf_op jit(solution)/shard_map/stack | solution.py:106
  118.8 2.3 %copy.249 = bf16[1,2,2,3,16,16]{5,4,3,2,1,0:T(8,128)(2,1)} copy(bf16[1,2,2,3,16,16]{1,5,4,3,2,0:T(8,128)(2,1)} %get-tuple-element.24) | data formatting | bytes 12288 | tf_op jit(solution)/shard_map/stack | solution.py:106
  121.1 2.3 %copy.250 = bf16[1,2,2,3,16,16]{5,4,3,2,1,0:T(8,128)(2,1)} copy(bf16[1,2,2,3,16,16]{1,5,4,3,2,0:T(8,128)(2,1)} %get-tuple-element.23) | data formatting | bytes 12288 | tf_op jit(solution)/shard_map/stack | solution.py:106
  123.4 2.3 %copy.251 = bf16[1,2,2,3,16,16]{5,4,3,2,1,0:T(8,128)(2,1)} copy(bf16[1,2,2,3,16,16]{1,5,4,3,2,0:T(8,128)(2,1)} %get-tuple-element.22) | data formatting | bytes 12288 | tf_op jit(solution)/shard_map/stack | solution.py:106
  125.7 2.3 %copy.252 = bf16[1,2,2,3,16,16]{5,4,3,2,1,0:T(8,128)(2,1)} copy(bf16[1,2,2,3,16,16]{1,5,4,3,2,0:T(8,128)(2,1)} %get-tuple-element.21) | data formatting | bytes 12288 | tf_op jit(solution)/shard_map/stack | solution.py:106
  128.0 2.3 %copy.253 = bf16[1,2,2,3,16,16]{5,4,3,2,1,0:T(8,128)(2,1)} copy(bf16[1,2,2,3,16,16]{1,5,4,3,2,0:T(8,128)(2,1)} %get-tuple-element.20) | data formatting | bytes 12288 | tf_op jit(solution)/shard_map/stack | solution.py:106
  130.3 2.3 %copy.254 = bf16[1,2,2,3,16,16]{5,4,3,2,1,0:T(8,128)(2,1)} copy(bf16[1,2,2,3,16,16]{1,5,4,3,2,0:T(8,128)(2,1)} %get-tuple-element.19) | data formatting | bytes 12288 | tf_op jit(solution)/shard_map/stack | solution.py:106
  132.6 2.3 %copy.255 = bf16[1,2,2,3,16,16]{5,4,3,2,1,0:T(8,128)(2,1)} copy(bf16[1,2,2,3,16,16]{1,5,4,3,2,0:T(8,128)(2,1)} %get-tuple-element.18) | data formatting | bytes 12288 | tf_op jit(solution)/shard_map/stack | solution.py:106
  134.9 2.3 %copy.256 = bf16[1,2,2,3,16,16]{5,4,3,2,1,0:T(8,128)(2,1)} copy(bf16[1,2,2,3,16,16]{1,5,4,3,2,0:T(8,128)(2,1)} %get-tuple-element.17) | data formatting | bytes 12288 | tf_op jit(solution)/shard_map/stack | solution.py:106
  159.6 2.0 %reshape.175 = bf16[16,2,1536]{2,1,0:T(2,128)(2,1)S(1)} reshape(bf16[16,2,2,3,16,16]{5,4,3,2,1,0:T(8,128)(2,1)} %constant_dynamic-update-slice_fusion) | data formatting | bytes 196608
  161.6 10.0 %all_to_all.23 = bf16[16,2,1536]{2,1,0:T(2,128)(2,1)S(1)} all-to-all(bf16[16,2,1536]{2,1,0:T(2,128)(2,1)S(1)} %reshape.175), channel_id=1, replica_groups=mesh['wheel'=16,'slab'=2] {'wheel'}, dimensions={0} | all-to-all | bytes 196608 | tf_op jit(solution)/shard_map/all_to_all | solution.py:105
  173.5 1.7 reshape_reshape.3
  (82 shorter events, 50.9 us)
Async XLA Ops:
  0.0 175.8 %copy-start = (bf16[1,8,384,384]{3,2,1,0:T(8,128)(2,1)S(1)}, bf16[1,8,384,384]{3,2,1,0:T(8,128)(2,1)}, u32[]{:S(2)}) copy-start(bf16[1,8,384,384]{3,2,1,0:T(8,128)(2,1)} %param.17) | copy-start | bytes 7077892
  0.0 27.1 %copy-start.1 = (f32[2,2,3,16,256]{4,3,2,1,0:T(8,128)S(1)}, f32[2,2,3,16,256]{4,3,2,1,0:T(8,128)}, u32[]{:S(2)}) copy-start(f32[2,2,3,16,256]{4,3,2,1,0:T(8,128)} %param.10) | copy-start | bytes 589828
  0.0 27.1 %copy-start.2 = (s32[8,256]{1,0:T(8,128)S(1)}, s32[8,256]{1,0:T(8,128)}, u32[]{:S(2)}) copy-start(s32[8,256]{1,0:T(8,128)} %param.12) | copy-start | bytes 24580
  0.0 27.7 %copy-start.3 = (f32[3,256]{1,0:T(4,128)S(1)}, f32[3,256]{1,0:T(4,128)}, u32[]{:S(2)}) copy-start(f32[3,256]{1,0:T(4,128)} %param.16) | copy-start | bytes 9220
  5.8 25.7 %collective-permute-start = (bf16[2,3,16,64]{3,2,1,0:T(8,128)(2,1)}, bf16[2,3,16,64]{3,2,1,0:T(8,128)(2,1)}, u32[]{:S(2)}, u32[]{:S(2)}) collective-permute-start(bf16[2,3,16,64]{3,2,1,0:T(8,128)(2,1)} %bitcast_convert_fusion.1), channel_id=1, source_target_pairs={{0,1},{2,3},{4,5},{6,7},{8,9},{10,11},{12,13},{14,15},{16,17},{18,... | collective-permute-start | bytes 36872 | tf_op jit(solution)/shard_map/ppermute | solution.py:21
  14.8 16.7 %collective-permute-start.1 = (bf16[2,3,16,64]{3,2,1,0:T(8,128)(2,1)}, bf16[2,3,16,64]{3,2,1,0:T(8,128)(2,1)}, u32[]{:S(2)}, u32[]{:S(2)}) collective-permute-start(bf16[2,3,16,64]{3,2,1,0:T(8,128)(2,1)} %bitcast_convert_fusion), channel_id=1, source_target_pairs={{1,0},{3,2},{5,4},{7,6},{9,8},{11,10},{13,12},{15,14},{17,16},{19,... | collective-permute-start | bytes 36872 | tf_op jit(solution)/shard_map/ppermute | solution.py:24
  20.0 12.5 %collective-permute-start.2 = (f32[3,16,64]{2,1,0:T(8,128)}, f32[3,16,64]{2,1,0:T(8,128)}, u32[]{:S(2)}, u32[]{:S(2)}) collective-permute-start(f32[3,16,64]{2,1,0:T(8,128)} %get-tuple-element.38), channel_id=1, source_target_pairs={{0,2},{2,4},{4,6},{6,8},{8,10},{10,12},{12,14},{14,16},{16,18},{18... | collective-permute-start | bytes 36872 | tf_op jit(solution)/shard_map/ppermute | solution.py:21
  22.6 10.7 %collective-permute-start.3 = (f32[3,16,64]{2,1,0:T(8,128)S(1)}, f32[3,16,64]{2,1,0:T(8,128)S(1)}, u32[]{:S(2)}, u32[]{:S(2)}) collective-permute-start(f32[3,16,64]{2,1,0:T(8,128)S(1)} %get-tuple-element.37), channel_id=1, source_target_pairs={{2,0},{4,2},{6,4},{8,6},{10,8},{12,10},{14,12},{16,14},{18,16},{20... | collective-permute-start | bytes 36872 | tf_op jit(solution)/shard_map/ppermute | solution.py:24
  78.0 12.5 %all-to-all-start = ((f32[16,1,3072]{2,1,0:T(1,128)}), f32[16,1,3072]{2,1,0:T(1,128)S(1)}, u32[]{:S(2)}, u32[]{:S(2)}) async-start(f32[16,1,3072]{2,1,0:T(1,128)} %reshape.173), calls=%async_computation | async-start | bytes 393216 | tf_op jit(solution)/shard_map/all_to_all | solution.py:95
